TPU v7x, 256 devices: a whole 4x4x8 slice. The times are simulated.
256 devices in a mesh: dp: 16 (over z, core), expert: 16 (over y, x).
Axes of the slice: x: 4, y: 4, z: 8, core: 2. Of those that a mesh axis runs over, the one named last changes fastest.
Arguments:
- tokens: bfloat16 [32768, 2048], P(('dp', 'expert')), may hold values from -6 to 6
- out_grad: bfloat16 [32768, 2048], P(('dp', 'expert')), may hold values from -1.5 to 1.5
- routes: int32 [32768, 2], P(('dp', 'expert')), may hold values from 0 to 15, all different within a row; in each aligned block of 128 rows (0 to 127, 128 to 255, ...) at most 32 rows name the same one
- route_probs: bfloat16 [32768, 2], P(('dp', 'expert')), may hold values from 0.049804688 to 1
- kept_count: int32 [16], P('dp'), may hold values from 512 to 2048, as said below
- gate_weight: bfloat16 [16, 2048, 768], P('expert', 'dp'), may hold values from -0.125 to 0.125
- up_weight: bfloat16 [16, 2048, 768], P('expert', 'dp'), may hold values from -0.125 to 0.125
- down_weight: bfloat16 [16, 2048, 768], P('expert', 'dp'), may hold values from -0.21875 to 0.21875
Outputs:
- token_grad: bfloat16 [32768, 2048], P(('dp', 'expert'))
- prob_grad: bfloat16 [32768, 2], P(('dp', 'expert'))
- weight_grad: bfloat16 [16, 2048, 2304], P('expert', 'dp')
Inputs may be any that keep to these rules, and one draw needn't show every extreme that they name: `routes`: among the rows of one device, no expert is named more than 32 times, and a row names 2 different experts. `kept_count`: rows of a data group whose index within the group is below its count are kept; in every draw some group keeps all its rows and another keeps a quarter of them.
All inputs are finite; a program needn't handle non-finite values.
Results may differ from a plain program's by a relative error of at most 0.018.
Values may be sent and summed in bfloat16 or wider, within the bound.
No kernel may reach another device: no remote copies, remote signals or barrier semaphores. Data moves between devices by JAX's collectives and lax.ppermute only.
A program may use at most 128 MiB of HBM per device.

v0:
```python
import jax
import jax.numpy as jnp
from jax import lax
from jax.sharding import PartitionSpec as P


def contract_rows(left, right):
    return lax.dot_general(
        left, right, (((0,), (0,)), ((), ())), preferred_element_type=jnp.float32
    )


def contract_last(left, right):
    return lax.dot_general(
        left, right, (((1,), (1,)), ((), ())), preferred_element_type=jnp.float32
    )


def per_device(
    tokens, out_grad, routes, route_probs, kept_count, gate_weight, up_weight, down_weight
):
    tok_rows, width = tokens.shape
    top = routes.shape[1]
    experts = lax.axis_size("expert")
    capacity = 2 * tok_rows * top // experts
    slots = experts * capacity
    weights = lax.all_gather(
        jnp.concatenate((gate_weight, up_weight, down_weight), axis=0), "dp", axis=1, tiled=True
    )
    row = lax.axis_index("expert") * tok_rows + jnp.arange(tok_rows, dtype=jnp.int32)
    kept = row < kept_count[0]
    masked = jnp.where(kept[:, None], out_grad, jnp.zeros_like(out_grad))
    flat = routes.reshape(-1)
    onehot = (flat[:, None] == jnp.arange(experts, dtype=jnp.int32)[None, :]).astype(jnp.int32)
    before = jnp.cumsum(onehot, axis=0) - onehot
    position = jnp.sum(before * onehot, axis=1)
    target = (flat * capacity + position).reshape(tok_rows, top)
    slot = jnp.arange(slots, dtype=jnp.int32)[:, None]
    probs = route_probs.astype(jnp.float32)
    match = [slot == target[None, :, k] for k in range(top)]
    placing = (match[0] | match[1]).astype(jnp.bfloat16)
    weighted = (
        jnp.where(match[0], probs[None, :, 0], 0.0) + jnp.where(match[1], probs[None, :, 1], 0.0)
    ).astype(jnp.bfloat16)
    send_rows = jnp.dot(placing, tokens, preferred_element_type=jnp.float32).astype(jnp.bfloat16)
    send_scaled = jnp.dot(weighted, masked, preferred_element_type=jnp.float32).astype(jnp.bfloat16)
    rows_in = lax.all_to_all(send_rows, "expert", split_axis=0, concat_axis=0, tiled=True)
    scaled = lax.all_to_all(send_scaled, "expert", split_axis=0, concat_axis=0, tiled=True)
    pre_gate = jnp.dot(rows_in, weights[0], preferred_element_type=jnp.float32)
    pre_up = jnp.dot(rows_in, weights[1], preferred_element_type=jnp.float32)
    sig = jax.nn.sigmoid(pre_gate)
    act = (pre_gate * sig * pre_up).astype(jnp.bfloat16)
    back_hidden = jnp.dot(scaled, weights[2], preferred_element_type=jnp.float32)
    prob_part = jnp.sum(act.astype(jnp.float32) * back_hidden, axis=1)
    d_gate = (back_hidden * pre_up * sig * (1.0 + pre_gate * (1.0 - sig))).astype(jnp.bfloat16)
    d_up = (back_hidden * pre_gate * sig).astype(jnp.bfloat16)
    weight_grad = lax.psum_scatter(
        jnp.concatenate(
            (
                contract_rows(rows_in, d_gate),
                contract_rows(rows_in, d_up),
                contract_rows(scaled, act),
            ),
            axis=1,
        ).astype(jnp.bfloat16),
        "dp",
        scatter_dimension=0,
        tiled=True,
    )[None]
    route_back = (contract_last(d_gate, weights[0]) + contract_last(d_up, weights[1])).astype(
        jnp.bfloat16
    )
    prob_all = lax.all_gather(
        prob_part.astype(jnp.bfloat16).reshape(experts, capacity), "expert", axis=0, tiled=False
    )
    rows_back = lax.all_to_all(route_back, "expert", split_axis=0, concat_axis=0, tiled=True)
    prob_back = lax.dynamic_index_in_dim(
        prob_all, lax.axis_index("expert"), axis=1, keepdims=False
    ).reshape(slots)
    token_grad = contract_rows(placing, rows_back).astype(jnp.bfloat16)
    prob_grad = jnp.stack(
        [jnp.sum(jnp.where(m, prob_back.astype(jnp.float32)[:, None], 0.0), axis=0) for m in match],
        axis=1,
    )
    prob_grad = (prob_grad / probs).astype(jnp.bfloat16)
    return (token_grad, prob_grad, weight_grad)


def solution(mesh):
    in_specs = (
        P(("dp", "expert"), None),
        P(("dp", "expert"), None),
        P(("dp", "expert"), None),
        P(("dp", "expert"), None),
        P("dp"),
        P("expert", "dp", None),
        P("expert", "dp", None),
        P("expert", "dp", None),
    )
    out_specs = (P(("dp", "expert"), None), P(("dp", "expert"), None), P("expert", "dp", None))
    return jax.shard_map(
        per_device, mesh=mesh, in_specs=in_specs, out_specs=out_specs, check_vma=False
    )
```

profile of v0, /device:TPU:8, one launch (start us, length us, event | category | flops | bytes accessed | tf_op | source)
XLA Modules:
  0.0 198.0 jit_solution(17751260392276215805)
XLA Ops:
  7.2 0.0 copy-start
  7.2 0.0 copy-start.2
  7.2 0.0 all-gather.2.cloned.1.call-start
  7.2 2.0 %pad_maximum_fusion.1 = bf16[3,128,768]{2,1,0:T(8,128)(2,1)} fusion(bf16[1,128,768]{2,1,0:T(8,128)(2,1)} %param.15, bf16[1,128,768]{2,1,0:T(8,128)(2,1)} %param.14, bf16[1,128,768]{2,1,0:T(8,128)(2,1)} %param.13), kind=kLoop, calls=%fused_computation.20 | loop fusion | flops 589824 | bytes 1179648 | tf_op jit(solution)/shard_map/concatenate | solution.py:28
  9.3 0.0 all-gather.2.cloned.1.call-update
  9.3 0.8 copy.36
  10.1 0.1 eq.56
  10.2 0.1 eq.60
  10.4 0.6 reduce-window.6
  11.0 0.2 slice_reduce_fusion
  11.2 0.1 fusion.21
  11.3 0.1 reduce_sum.39
  11.4 0.1 copy.39
  11.5 0.0 copy-done.2
  11.5 0.0 copy-done
  11.6 2.0 %convolution_convert_fusion.4 = bf16[512,2048]{1,0:T(8,128)(2,1)} fusion(bf16[128,2048]{1,0:T(8,128)(2,1)S(1)} %copy-done, s32[128]{0:T(128)S(1)} %get-tuple-element.30, s32[128]{0:T(128)S(1)} %get-tuple-element.29), kind=kOutput, calls=%fused_computation.10 | convolution fusion | flops 269680640 | bytes 2622464 | tf_op jit(solution)/shard_map/dot_general | solution.py:45
  13.6 7.5 %all-to-all-start.1 = ((bf16[16,32,2048]{2,1,0:T(8,128)(2,1)}), bf16[16,32,2048]{2,1,0:T(8,128)(2,1)S(1)}, u32[]{:S(2)}, u32[]{:S(2)}) async-start(bf16[16,32,2048]{2,1,0:T(8,128)(2,1)} %bitcast.9), calls=%async_computation.1 | async-start | bytes 4194304 | tf_op jit(solution)/shard_map/all_to_all | solution.py:47
  21.7 0.0 copy-done.3
  21.8 2.2 %convolution_convert_fusion.3 = bf16[512,2048]{1,0:T(8,128)(2,1)} fusion(bf16[128,2048]{1,0:T(8,128)(2,1)S(1)} %copy-done.1, pred[128]{0:T(512)(128)(4,1)S(1)} %add_compare_fusion, f32[128]{0:T(128)S(1)} %get-tuple-element.28, f32[128]{0:T(128)S(1)} %get-tuple-element.27, s32[128]{0:T(128)S(1)} %get-tuple-element.30, s32[128]{0:T(128)S(1)} %get-tuple-element.29), kind=kOutput, calls=%fused_computation.9 | convolution fusion | flops 270139392 | bytes 2623616 | tf_op jit(solution)/shard_map/dot_general | solution.py:46
  24.0 27.5 %all-to-all-done.1 = bf16[16,32,2048]{2,1,0:T(8,128)(2,1)S(1)} async-done(((bf16[16,32,2048]{2,1,0:T(8,128)(2,1)}), bf16[16,32,2048]{2,1,0:T(8,128)(2,1)S(1)}, u32[]{:S(2)}, u32[]{:S(2)}) %all-to-all-start.1) | async-done | bytes 2097184 | tf_op jit(solution)/shard_map/all_to_all | solution.py:47
  51.5 5.6 %all-to-all-start = ((bf16[16,32,2048]{2,1,0:T(8,128)(2,1)}), bf16[16,32,2048]{2,1,0:T(8,128)(2,1)}, u32[]{:S(2)}, u32[]{:S(2)}) async-start(bf16[16,32,2048]{2,1,0:T(8,128)(2,1)} %bitcast.6), calls=%async_computation | async-start | bytes 4194304 | tf_op jit(solution)/shard_map/all_to_all | solution.py:48
  57.1 0.2 reduce-scatter.4.cloned.1.call-start
  57.3 16.9 %all-gather.2.cloned.1.call-done = bf16[3,2048,768]{2,1,0:T(8,128)(2,1)} async-done(((bf16[3,128,768]{2,1,0:T(8,128)(2,1)}), bf16[3,2048,768]{2,1,0:T(8,128)(2,1)}) %all-gather.2.cloned.1.call-update) | async-done | bytes 9437200 | tf_op jit(solution)/shard_map/all_gather | solution.py:27
  74.2 4.8 %fusion.1 = f32[512,768]{1,0:T(8,128)} fusion(bf16[512,2048]{1,0:T(8,128)(2,1)S(1)} %bitcast.67, bf16[3,2048,768]{2,1,0:T(8,128)(2,1)} %all-gather.2.cloned.1.call-done), kind=kOutput, calls=%fused_computation.11 | convolution fusion | flops 1610612736 | bytes 6815744 | tf_op jit(solution)/shard_map/dot_general | solution.py:50
  79.1 4.9 %fusion.3 = f32[512,768]{1,0:T(8,128)} fusion(bf16[512,2048]{1,0:T(8,128)(2,1)S(1)} %bitcast.68, bf16[3,2048,768]{2,1,0:T(8,128)(2,1)} %all-gather.2.cloned.1.call-done), kind=kOutput, calls=%fused_computation.13 | convolution fusion | flops 1610612736 | bytes 6815744 | tf_op jit(solution)/shard_map/dot_general | solution.py:49
  83.9 0.8 all-to-all-done
  84.7 5.8 %multiply_reduce_fusion = (bf16[512]{0:T(512)(128)(2,1)S(1)}, bf16[512,768]{1,0:T(8,128)(2,1)S(1)}, bf16[512,768]{1,0:T(8,128)(2,1)S(1)}, bf16[512,768]{1,0:T(8,128)(2,1)S(1)}) fusion(f32[512,768]{1,0:T(8,128)} %fusion.1, f32[512,768]{1,0:T(8,128)} %fusion.3, bf16[512,2048]{1,0:T(8,128)(2,1)} %bitcast.7, bf16[3,2048,768]{2,1,0:T(8,128)(2,1)} %all-gather.2.cloned.1.call-done), kind=kOutput, calls=%fused_computation.15 | convolution fusion | flops 1618083328 | bytes 10748928 | tf_op jit(solution)/shard_map/dot_general | solution.py:53
  90.6 3.7 %convolution_convert_fusion = bf16[2048,768]{0,1:T(8,128)(2,1)S(1)} fusion(bf16[512,2048]{1,0:T(8,128)(2,1)} %bitcast.7, bf16[512,768]{1,0:T(8,128)(2,1)S(1)} %get-tuple-element.24), kind=kOutput, calls=%fused_computation.2 | convolution fusion | flops 1612185600 | bytes 6029312 | tf_op jit(solution)/shard_map/dot_general | solution.py:8
  94.3 1.9 convolution_convert_fusion.1
  96.2 0.0 copy-done.4
  96.2 1.9 convolution_convert_fusion.2
  98.1 4.7 %pad_maximum_fusion = bf16[2048,2304]{0,1:T(8,128)(2,1)} fusion(bf16[2048,768]{0,1:T(8,128)(2,1)S(1)} %convolution_convert_fusion, bf16[2048,768]{0,1:T(8,128)(2,1)S(1)} %convolution_convert_fusion.1, bf16[2048,768]{0,1:T(8,128)(2,1)S(1)} %convolution_convert_fusion.2), kind=kLoop, calls=%fused_computation | loop fusion | flops 28311552 | bytes 18874368 | tf_op jit(solution)/shard_map/concatenate | solution.py:58
  102.7 12.2 %copy.41 = bf16[2048,2304]{1,0:T(8,128)(2,1)} copy(bf16[2048,2304]{0,1:T(8,128)(2,1)} %pad_maximum_fusion) | data formatting | bytes 18874368
  114.9 0.0 reduce-scatter.4.cloned.1.call-update
  115.0 1.1 copy-done.5
  116.1 3.7 %fusion.2 = f32[512,2048]{1,0:T(8,128)S(1)} fusion(bf16[512,768]{1,0:T(8,128)(2,1)S(1)} %copy-done.5, bf16[3,2048,768]{2,1,0:T(8,128)(2,1)} %all-gather.2.cloned.1.call-done), kind=kOutput, calls=%fused_computation.12 | convolution fusion | flops 1610612736 | bytes 8126464 | tf_op jit(solution)/shard_map/dot_general | solution.py:14
  119.8 5.0 %add_convert_fusion = bf16[512,2048]{1,0:T(8,128)(2,1)} fusion(f32[512,2048]{1,0:T(8,128)S(1)} %fusion.2, bf16[512,768]{1,0:T(8,128)(2,1)S(1)} %get-tuple-element.26, bf16[3,2048,768]{2,1,0:T(8,128)(2,1)} %all-gather.2.cloned.1.call-done), kind=kOutput, calls=%fused_computation.1 | convolution fusion | flops 1612709888 | bytes 10223616 | tf_op jit(solution)/shard_map/dot_general | solution.py:14
  124.8 6.4 %all-to-all-start.2 = ((bf16[16,32,2048]{2,1,0:T(8,128)(2,1)}), bf16[16,32,2048]{2,1,0:T(8,128)(2,1)S(1)}, u32[]{:S(2)}, u32[]{:S(2)}) async-start(bf16[16,32,2048]{2,1,0:T(8,128)(2,1)} %bitcast.71), calls=%async_computation.2 | async-start | bytes 4194304 | tf_op jit(solution)/shard_map/all_to_all | solution.py:76
  131.3 0.1 convert_element_type.79
  131.4 44.6 %all_gather.7 = bf16[16,16,32]{2,1,0:T(8,128)(2,1)S(1)} all-gather(bf16[1,16,32]{2,1,0:T(8,128)(2,1)S(1)} %convert_element_type.79), channel_id=1, replica_groups=mesh['dp'=16,'expert'=16] {'expert'}, dimensions={0}, use_global_device_ids=true | all-gather | bytes 17408 | tf_op jit(solution)/shard_map/all_gather | solution.py:73
  176.0 0.1 reshape.62
  176.1 0.2 select_reduce_fusion.1
  176.3 0.5 fusion.23
  176.8 0.0 all-to-all-done.2
  176.8 1.3 convolution_convert_fusion.5
  178.1 10.7 %reduce-scatter.4.cloned.1.call-done = bf16[128,2304]{1,0:T(8,128)(2,1)} async-done(((bf16[2048,2304]{1,0:T(8,128)(2,1)}), bf16[128,2304]{1,0:T(8,128)(2,1)}) %reduce-scatter.4.cloned.1.call-update) | async-done | bytes 589840
  188.8 1.4 copy.42
  190.1 1.1 copy.40
  (14 shorter events, 0.1 us)
Async XLA Ops:
  7.2 4.4 %copy-start = (bf16[128,2048]{1,0:T(8,128)(2,1)S(1)}, bf16[128,2048]{1,0:T(8,128)(2,1)}, u32[]{:S(2)}) copy-start(bf16[128,2048]{1,0:T(8,128)(2,1)} %param.8) | copy-start | bytes 1572868
  7.2 4.3 %copy-start.2 = (s32[128,2]{0,1:T(2,128)S(1)}, s32[128,2]{0,1:T(2,128)}, u32[]{:S(2)}) copy-start(s32[128,2]{0,1:T(2,128)} %param.10) | copy-start | bytes 3076
  7.2 67.0 %all-gather.2.cloned.1.call-start = ((), (), s32[]{:S(2)}) async-start(), calls=%async_computation.4 | async-start | bytes 10027008 | tf_op jit(solution)/shard_map/all_gather | solution.py:27
  13.6 8.2 %copy-start.3 = (bf16[128,2]{0,1:T(2,128)(2,1)S(1)}, bf16[128,2]{0,1:T(2,128)(2,1)}, u32[]{:S(2)}) copy-start(bf16[128,2]{0,1:T(2,128)(2,1)} %param.11) | copy-start | bytes 1540
  13.6 8.2 %copy-start.1 = (bf16[128,2048]{1,0:T(8,128)(2,1)S(1)}, bf16[128,2048]{1,0:T(8,128)(2,1)}, u32[]{:S(2)}) copy-start(bf16[128,2048]{1,0:T(8,128)(2,1)} %param.9) | copy-start | bytes 1572868
  13.6 37.9 %all-to-all-start.1 = ((bf16[16,32,2048]{2,1,0:T(8,128)(2,1)}), bf16[16,32,2048]{2,1,0:T(8,128)(2,1)S(1)}, u32[]{:S(2)}, u32[]{:S(2)}) async-start(bf16[16,32,2048]{2,1,0:T(8,128)(2,1)} %bitcast.9), calls=%async_computation.1 | async-start | bytes 4194304 | tf_op jit(solution)/shard_map/all_to_all | solution.py:47
  51.5 33.3 %all-to-all-start = ((bf16[16,32,2048]{2,1,0:T(8,128)(2,1)}), bf16[16,32,2048]{2,1,0:T(8,128)(2,1)}, u32[]{:S(2)}, u32[]{:S(2)}) async-start(bf16[16,32,2048]{2,1,0:T(8,128)(2,1)} %bitcast.6), calls=%async_computation | async-start | bytes 4194304 | tf_op jit(solution)/shard_map/all_to_all | solution.py:48
  57.1 131.7 %reduce-scatter.4.cloned.1.call-start = ((), (), s32[]{:S(2)}) async-start(), calls=%async_computation.5 | async-start | bytes 10027008
  90.6 5.6 %copy-start.4 = (bf16[512,768]{1,0:T(8,128)(2,1)}, bf16[512,768]{1,0:T(8,128)(2,1)S(1)}, u32[]{:S(2)}) copy-start(bf16[512,768]{1,0:T(8,128)(2,1)S(1)} %get-tuple-element.25) | copy-start | bytes 2359300
  114.9 1.1 copy-start.5
  124.8 51.9 %all-to-all-start.2 = ((bf16[16,32,2048]{2,1,0:T(8,128)(2,1)}), bf16[16,32,2048]{2,1,0:T(8,128)(2,1)S(1)}, u32[]{:S(2)}, u32[]{:S(2)}) async-start(bf16[16,32,2048]{2,1,0:T(8,128)(2,1)} %bitcast.71), calls=%async_computation.2 | async-start | bytes 4194304 | tf_op jit(solution)/shard_map/all_to_all | solution.py:76
Sparse Core Ops, SparseCore 0:
  10.4 63.7 all-gather.1
  115.1 73.6 reduce-scatter.3
where the time goes:
time: 199 us; the launch traced here: 198 us
  waiting for transfers between devices  55.9 us (28%)
  blocking collectives  44.6 us (22%)
  matrix products  37.2 us (19%)
  starting transfers between devices  19.8 us (10%)
  local copies, waits for them, and re-layouts  17.4 us (9%)
  between operations  14.8 us (7%)
  other arithmetic  8.16 us (4%)
    all_gather x1, blocking collectives, per_device(): lax.all_gather(prob_part.astype(jnp.bfloat16).reshape(experts, capacity),...  44.6 us
    all_to_all x1, waiting for transfers between devices, per_device(): lax.all_to_all(send_rows, 'expert', split_axis=0, concat_axis=0, tiled=True)  27.5 us
    all_gather x1, waiting for transfers between devices, per_device(): lax.all_gather(jnp.concatenate((gate_weight, up_weight, down_weight), axi...  16.9 us
    unnamed x16, local copies, waits for them, and re-layouts  16.6 us
    unnamed x3, waiting for transfers between devices  10.7 us
    dot_general x2, matrix products, contract_last(): lax.dot_general(left, right, (((1,), (1,)), ((), ())), preferred_element_...  8.76 us
    dot_general x4, matrix products, contract_rows(): lax.dot_general(left, right, (((0,), (0,)), ((), ())), preferred_element_...  8.75 us
    all_to_all x1, starting transfers between devices, per_device(): lax.all_to_all(send_rows, 'expert', split_axis=0, concat_axis=0, tiled=True)  7.52 us
  transfers between devices with their start and end apart: 5, of which 4 were waited for; matrix products, arithmetic and copies ran while one was open for 14% of the time, Pallas kernels for 0%

commit v1 on v0

--- a/solution.py
+++ b/solution.py
@@ -24,9 +24,11 @@
     experts = lax.axis_size("expert")
     capacity = 2 * tok_rows * top // experts
     slots = experts * capacity
-    weights = lax.all_gather(
-        jnp.concatenate((gate_weight, up_weight, down_weight), axis=0), "dp", axis=1, tiled=True
-    )
+    block = jnp.concatenate((gate_weight, up_weight, down_weight), axis=0)
+    count = lax.axis_size("dp")
+    blocks = jnp.stack([block for _ in range(count)])
+    blocks = lax.all_to_all(blocks, "dp", split_axis=0, concat_axis=0)
+    weights = jnp.concatenate(blocks, axis=1)
     row = lax.axis_index("expert") * tok_rows + jnp.arange(tok_rows, dtype=jnp.int32)
     kept = row < kept_count[0]
     masked = jnp.where(kept[:, None], out_grad, jnp.zeros_like(out_grad))

time: 199 us -> 419 us (2.11)
  waiting for transfers between devices: 55.9 us -> 268 us
  local copies, waits for them, and re-layouts: 17.4 us -> 28.2 us
  starting transfers between devices: 19.8 us -> 27.1 us
  matrix products: 37.2 us -> 32 us
    all_to_all x0 -> x1, waiting for transfers between devices: none -> 204 us  [per_device(): blocks = lax.all_to_all(blocks, 'dp', split_axis=0, concat_axis=0)]
    all_to_all x1, waiting for transfers between devices: 0.82 us -> 19 us  [per_device(): lax.all_to_all(send_scaled, 'expert', split_axis=0, concat_axis=0, tiled=...]
    all_gather x1 -> x0, waiting for transfers between devices: 16.9 us -> none  [per_device(): lax.all_gather(jnp.concatenate((gate_weight, up_weight, down_weight), axi...]
    all_to_all x0 -> x1, starting transfers between devices: none -> 8.74 us  [per_device(): blocks = lax.all_to_all(blocks, 'dp', split_axis=0, concat_axis=0)]
    slice x1 -> x2, local copies, waits for them, and re-layouts: 0.18 us -> 5.55 us  [the longest x1 5.36 us: per_device(): pre_up = jnp.dot(rows_in, weights[1], preferred_element_type=jnp.float32)]
    another operation x1 -> x2, local copies, waits for them, and re-layouts: 0.01 us -> 4.76 us  [the longest x1 4.76 us: per_device(): blocks = jnp.stack([block for _ in range(count)])]
    unnamed x3 -> x2, waiting for transfers between devices: 10.7 us -> 15 us
    unnamed x16 -> x32, local copies, waits for them, and re-layouts: 16.6 us -> 17.3 us
  transfers between devices with their start and end apart: 5 -> 5, of which waited for: 4 -> 4; matrix products, arithmetic and copies ran while one was open for 14% -> 5% of each run, Pallas kernels for 0% -> 0%
where the time goes in v1:
time: 419 us
  waiting for transfers between devices  268 us (64%)
  blocking collectives  41.6 us (10%)
  matrix products  32 us (8%)
  local copies, waits for them, and re-layouts  28.2 us (7%)
  starting transfers between devices  27.1 us (6%)
  between operations  14.9 us (4%)
  other arithmetic  6.65 us (2%)
    all_to_all x1, waiting for transfers between devices, per_device(): blocks = lax.all_to_all(blocks, 'dp', split_axis=0, concat_axis=0)  204 us
    all_gather x1, blocking collectives, per_device(): lax.all_gather(prob_part.astype(jnp.bfloat16).reshape(experts, capacity),...  41.6 us
    all_to_all x1, waiting for transfers between devices, per_device(): lax.all_to_all(send_rows, 'expert', split_axis=0, concat_axis=0, tiled=True)  30.3 us
    all_to_all x1, waiting for transfers between devices, per_device(): lax.all_to_all(send_scaled, 'expert', split_axis=0, concat_axis=0, tiled=...  19 us
    unnamed x32, local copies, waits for them, and re-layouts  17.3 us
    unnamed x2, waiting for transfers between devices  15 us
    dot_general x4, matrix products, contract_rows(): lax.dot_general(left, right, (((0,), (0,)), ((), ())), preferred_element_...  9 us
    all_to_all x1, starting transfers between devices, per_device(): blocks = lax.all_to_all(blocks, 'dp', split_axis=0, concat_axis=0)  8.74 us
  transfers between devices with their start and end apart: 5, of which 4 were waited for; matrix products, arithmetic and copies ran while one was open for 5% of the time, Pallas kernels for 0%

profile of v1, /device:TPU:8, one launch (start us, length us, event | category | flops | bytes accessed | tf_op | source)
XLA Modules:
  0.0 418.6 jit_solution(15802599485410447078)
XLA Ops:
  7.2 0.0 copy-start
  7.2 0.8 copy.36
  8.0 0.1 eq.56
  8.2 0.1 eq.60
  8.3 0.6 reduce-window.6
  8.9 0.2 slice_reduce_fusion
  9.1 0.1 fusion.17
  9.2 0.1 reduce_sum.39
  9.4 0.1 copy.39
  9.4 0.7 multiply_add_fusion
  10.2 0.0 copy-done
  10.2 2.0 convolution_convert_fusion.4
  12.2 7.5 %all-to-all-start.2 = ((bf16[16,32,2048]{2,1,0:T(8,128)(2,1)}), bf16[16,32,2048]{2,1,0:T(8,128)(2,1)S(1)}, u32[]{:S(2)}, u32[]{:S(2)}) async-start(bf16[16,32,2048]{2,1,0:T(8,128)(2,1)} %bitcast.10), calls=%async_computation.2 | async-start | bytes 4194304 | tf_op jit(solution)/shard_map/all_to_all | solution.py:49
  19.7 0.0 copy-done.6
  19.7 0.0 copy-done.7
  19.7 0.1 pad_maximum_fusion.1
  19.8 30.3 %all-to-all-done.2 = bf16[16,32,2048]{2,1,0:T(8,128)(2,1)S(1)} async-done(((bf16[16,32,2048]{2,1,0:T(8,128)(2,1)}), bf16[16,32,2048]{2,1,0:T(8,128)(2,1)S(1)}, u32[]{:S(2)}, u32[]{:S(2)}) %all-to-all-start.2) | async-done | bytes 2097184 | tf_op jit(solution)/shard_map/all_to_all | solution.py:49
  50.1 4.8 %stack.8 = bf16[16,3,128,768]{3,2,1,0:T(8,128)(2,1)} broadcast(bf16[3,128,768]{2,1,0:T(8,128)(2,1)S(1)} %pad_maximum_fusion.1), dimensions={1,2,3} | broadcast | bytes 10027008 | tf_op jit(solution)/shard_map/stack | solution.py:29
  54.9 8.7 %all-to-all-start.1 = ((bf16[16,3,128,768]{3,2,1,0:T(8,128)(2,1)}), bf16[16,3,128,768]{3,2,1,0:T(8,128)(2,1)}, u32[]{:S(2)}, u32[]{:S(2)}) async-start(bf16[16,3,128,768]{3,2,1,0:T(8,128)(2,1)} %stack.8), calls=%async_computation.1 | async-start | bytes 18874368 | tf_op jit(solution)/shard_map/all_to_all | solution.py:30
  64.3 2.1 convolution_convert_fusion.3
  66.5 203.8 %all-to-all-done.1 = bf16[16,3,128,768]{3,2,1,0:T(8,128)(2,1)} async-done(((bf16[16,3,128,768]{3,2,1,0:T(8,128)(2,1)}), bf16[16,3,128,768]{3,2,1,0:T(8,128)(2,1)}, u32[]{:S(2)}, u32[]{:S(2)}) %all-to-all-start.1) | async-done | bytes 9437216 | tf_op jit(solution)/shard_map/all_to_all | solution.py:30
  270.3 5.6 %all-to-all-start = ((bf16[16,32,2048]{2,1,0:T(8,128)(2,1)}), bf16[16,32,2048]{2,1,0:T(8,128)(2,1)}, u32[]{:S(2)}, u32[]{:S(2)}) async-start(bf16[16,32,2048]{2,1,0:T(8,128)(2,1)} %bitcast.6), calls=%async_computation | async-start | bytes 4194304 | tf_op jit(solution)/shard_map/all_to_all | solution.py:50
  275.8 0.2 reduce-scatter.4.cloned.1.call-start
  276.0 5.4 %fusion.22 = (bf16[1,16,128,768]{3,2,0,1:T(8,128)(2,1)S(1)}, bf16[1,16,128,768]{3,2,0,1:T(8,128)(2,1)S(1)}, bf16[1,16,128,768]{3,2,0,1:T(8,128)(2,1)}) fusion(bf16[3,16,128,768]{3,2,0,1:T(8,128)(2,1)} %bitcast.8), kind=kLoop, calls=%fused_computation.52 | loop fusion | bytes 18874368 | tf_op jit(solution)/shard_map/slice | solution.py:52
  281.4 3.1 fusion.23
  284.5 2.9 fusion.24
  287.5 19.0 %all-to-all-done = bf16[16,32,2048]{2,1,0:T(8,128)(2,1)} async-done(((bf16[16,32,2048]{2,1,0:T(8,128)(2,1)}), bf16[16,32,2048]{2,1,0:T(8,128)(2,1)}, u32[]{:S(2)}, u32[]{:S(2)}) %all-to-all-start) | async-done | bytes 2097184 | tf_op jit(solution)/shard_map/all_to_all | solution.py:50
  306.5 5.8 %multiply_reduce_fusion = (bf16[512]{0:T(512)(128)(2,1)S(1)}, bf16[512,768]{1,0:T(8,128)(2,1)S(1)}, bf16[512,768]{1,0:T(8,128)(2,1)S(1)}, bf16[512,768]{1,0:T(8,128)(2,1)S(1)}) fusion(f32[512,768]{1,0:T(8,128)} %fusion.23, f32[512,768]{1,0:T(8,128)} %fusion.24, bf16[512,2048]{1,0:T(8,128)(2,1)} %bitcast.7, bf16[2048,768]{1,0:T(8,128)(2,1)} %bitcast.66), kind=kOutput, calls=%fused_computation.8 | convolution fusion | flops 1618083328 | bytes 10748928 | tf_op jit(solution)/shard_map/dot_general | solution.py:55
  312.3 4.0 convolution_convert_fusion
  316.3 1.9 convolution_convert_fusion.1
  318.2 1.9 convolution_convert_fusion.2
  320.0 4.4 %pad_maximum_fusion = bf16[2048,2304]{0,1:T(8,128)(2,1)} fusion(bf16[2048,768]{0,1:T(8,128)(2,1)S(1)} %convolution_convert_fusion, bf16[2048,768]{0,1:T(8,128)(2,1)S(1)} %convolution_convert_fusion.1, bf16[2048,768]{0,1:T(8,128)(2,1)S(1)} %convolution_convert_fusion.2), kind=kLoop, calls=%fused_computation | loop fusion | flops 28311552 | bytes 18874368 | tf_op jit(solution)/shard_map/concatenate | solution.py:60
  324.5 12.8 %copy.41 = bf16[2048,2304]{1,0:T(8,128)(2,1)} copy(bf16[2048,2304]{0,1:T(8,128)(2,1)} %pad_maximum_fusion) | data formatting | bytes 18874368
  337.3 0.0 reduce-scatter.4.cloned.1.call-update
  337.3 1.1 copy-done.13
  338.4 3.9 fusion.25
  342.3 3.1 add_convert_fusion
  345.4 5.1 %all-to-all-start.3 = ((bf16[16,32,2048]{2,1,0:T(8,128)(2,1)}), bf16[16,32,2048]{2,1,0:T(8,128)(2,1)S(1)}, u32[]{:S(2)}, u32[]{:S(2)}) async-start(bf16[16,32,2048]{2,1,0:T(8,128)(2,1)} %bitcast.72), calls=%async_computation.3 | async-start | bytes 4194304 | tf_op jit(solution)/shard_map/all_to_all | solution.py:78
  350.5 0.1 convert_element_type.79
  350.6 41.6 %all_gather.3 = bf16[16,16,32]{2,1,0:T(8,128)(2,1)S(1)} all-gather(bf16[1,16,32]{2,1,0:T(8,128)(2,1)S(1)} %convert_element_type.79), channel_id=1, replica_groups=mesh['dp'=16,'expert'=16] {'expert'}, dimensions={0}, use_global_device_ids=true | all-gather | bytes 17408 | tf_op jit(solution)/shard_map/all_gather | solution.py:75
  392.2 0.1 reshape.75
  392.3 0.2 select_reduce_fusion.1
  392.5 0.5 fusion.19
  393.0 0.0 all-to-all-done.3
  393.0 1.3 convolution_convert_fusion.5
  394.3 15.0 %reduce-scatter.4.cloned.1.call-done = bf16[128,2304]{1,0:T(8,128)(2,1)} async-done(((bf16[2048,2304]{1,0:T(8,128)(2,1)}), bf16[128,2304]{1,0:T(8,128)(2,1)}) %reduce-scatter.4.cloned.1.call-update) | async-done | bytes 589840
  409.3 1.4 copy.42
  410.6 1.1 copy.40
  (31 shorter events, 0.1 us)
Async XLA Ops:
  7.2 3.0 copy-start
  10.2 9.6 %copy-start.6 = (bf16[1,128,768]{2,1,0:T(8,128)(2,1)S(1)}, bf16[1,128,768]{2,1,0:T(8,128)(2,1)}, u32[]{:S(2)}) copy-start(bf16[1,128,768]{2,1,0:T(8,128)(2,1)} %param.15) | copy-start | bytes 589828
  12.2 7.5 %copy-start.7 = (bf16[1,128,768]{2,1,0:T(8,128)(2,1)S(1)}, bf16[1,128,768]{2,1,0:T(8,128)(2,1)}, u32[]{:S(2)}) copy-start(bf16[1,128,768]{2,1,0:T(8,128)(2,1)} %param.14) | copy-start | bytes 589828
  12.2 7.5 %copy-start.8 = (bf16[1,128,768]{2,1,0:T(8,128)(2,1)S(1)}, bf16[1,128,768]{2,1,0:T(8,128)(2,1)}, u32[]{:S(2)}) copy-start(bf16[1,128,768]{2,1,0:T(8,128)(2,1)} %param.13) | copy-start | bytes 589828
  12.2 37.9 %all-to-all-start.2 = ((bf16[16,32,2048]{2,1,0:T(8,128)(2,1)}), bf16[16,32,2048]{2,1,0:T(8,128)(2,1)S(1)}, u32[]{:S(2)}, u32[]{:S(2)}) async-start(bf16[16,32,2048]{2,1,0:T(8,128)(2,1)} %bitcast.10), calls=%async_computation.2 | async-start | bytes 4194304 | tf_op jit(solution)/shard_map/all_to_all | solution.py:49
  54.9 9.4 %copy-start.9 = (bf16[128,2]{0,1:T(2,128)(2,1)S(1)}, bf16[128,2]{0,1:T(2,128)(2,1)}, u32[]{:S(2)}) copy-start(bf16[128,2]{0,1:T(2,128)(2,1)} %param.11) | copy-start | bytes 1540
  54.9 9.5 %copy-start.5 = (bf16[128,2048]{1,0:T(8,128)(2,1)S(1)}, bf16[128,2048]{1,0:T(8,128)(2,1)}, u32[]{:S(2)}) copy-start(bf16[128,2048]{1,0:T(8,128)(2,1)} %param.9) | copy-start | bytes 1572868
  54.9 215.4 %all-to-all-start.1 = ((bf16[16,3,128,768]{3,2,1,0:T(8,128)(2,1)}), bf16[16,3,128,768]{3,2,1,0:T(8,128)(2,1)}, u32[]{:S(2)}, u32[]{:S(2)}) async-start(bf16[16,3,128,768]{3,2,1,0:T(8,128)(2,1)} %stack.8), calls=%async_computation.1 | async-start | bytes 18874368 | tf_op jit(solution)/shard_map/all_to_all | solution.py:30
  270.3 36.2 %all-to-all-start = ((bf16[16,32,2048]{2,1,0:T(8,128)(2,1)}), bf16[16,32,2048]{2,1,0:T(8,128)(2,1)}, u32[]{:S(2)}, u32[]{:S(2)}) async-start(bf16[16,32,2048]{2,1,0:T(8,128)(2,1)} %bitcast.6), calls=%async_computation | async-start | bytes 4194304 | tf_op jit(solution)/shard_map/all_to_all | solution.py:50
  275.8 133.5 %reduce-scatter.4.cloned.1.call-start = ((), (), s32[]{:S(2)}) async-start(), calls=%async_computation.5 | async-start | bytes 10027008
  281.4 3.1 copy-start.2
  281.4 3.1 copy-start.4
  312.3 4.0 copy-start.10
  312.3 5.9 %copy-start.12 = (bf16[512,768]{1,0:T(8,128)(2,1)}, bf16[512,768]{1,0:T(8,128)(2,1)S(1)}, u32[]{:S(2)}) copy-start(bf16[512,768]{1,0:T(8,128)(2,1)S(1)} %get-tuple-element.28) | copy-start | bytes 2359300
  337.3 1.1 copy-start.13
  338.4 3.9 copy-start.3
  338.4 3.9 copy-start.11
  345.4 47.5 %all-to-all-start.3 = ((bf16[16,32,2048]{2,1,0:T(8,128)(2,1)}), bf16[16,32,2048]{2,1,0:T(8,128)(2,1)S(1)}, u32[]{:S(2)}, u32[]{:S(2)}) async-start(bf16[16,32,2048]{2,1,0:T(8,128)(2,1)} %bitcast.72), calls=%async_computation.3 | async-start | bytes 4194304 | tf_op jit(solution)/shard_map/all_to_all | solution.py:78
  350.5 61.2 %copy-start.1 = (bf16[128,2048]{1,0:T(8,128)(2,1)S(1)}, bf16[128,2048]{1,0:T(8,128)(2,1)}, u32[]{:S(2)}) copy-start(bf16[128,2048]{1,0:T(8,128)(2,1)} %param.8) | copy-start | bytes 1572868
Sparse Core Ops, SparseCore 0:
  337.4 71.7 reduce-scatter.3
